TPU v7x, 32 devices: a whole 2x2x4 slice. The times are simulated.
32 devices in a mesh: chan: 4 (over x, core), seq: 8 (over z, y).
Axes of the slice: x: 2, y: 2, z: 4, core: 2. Of those that a mesh axis runs over, the one named last changes fastest.
Arguments:
- query: bfloat16 [4096, 512], P('seq', 'chan'), may hold values from -6 to 6
- key: bfloat16 [4096, 512], P('seq', 'chan'), may hold values from -6 to 6
- value: bfloat16 [4096, 512], P('seq', 'chan'), may hold values from -6 to 6
- filter_weights: bfloat16 [512, 8, 512], P('chan', 'seq'), may hold values from -6 to 6
- skip_gain: float32 [512], P('chan'), may hold values from 0.5 to 1.5
- cotangent: bfloat16 [4096, 512], P('seq', 'chan'), may hold values from -6 to 6
Outputs:
- mixed: bfloat16 [4096, 512], P('seq', 'chan')
- query_grad: bfloat16 [4096, 512], P('seq', 'chan')
- key_grad: bfloat16 [4096, 512], P('seq', 'chan')
- value_grad: bfloat16 [4096, 512], P('seq', 'chan')
- filter_grad: float32 [512, 8, 512], P('chan', 'seq')
All inputs are finite; a program needn't handle non-finite values.
Results may differ from a plain program's by a relative error of at most 0.0085.
Values may be sent and summed in bfloat16 or wider, within the bound.
A program may use at most 64 MiB of HBM per device.

v0:
```python
import functools
import math

import jax
import jax.numpy as jnp
import numpy as np
from jax import lax
from jax.experimental import pallas as pl
from jax.experimental.pallas import tpu as pltpu
from jax.sharding import PartitionSpec as P

MESH = pl.DeviceIdType.MESH
F32 = jnp.float32
BF16 = jnp.bfloat16


def whole_vmem(count):
    return [pl.BlockSpec(memory_space=pltpu.VMEM)] * count


def split_table(table):
    high = jnp.asarray(table, F32).astype(BF16)
    low = (jnp.asarray(table, F32) - high.astype(F32)).astype(BF16)
    return high, low


def split_value(x):
    high = x.astype(BF16)
    return high, (x - high.astype(F32)).astype(BF16)


def dot(a, b):
    return jnp.dot(a, b, preferred_element_type=F32)


def tables(slow, fast, factor):
    length = 2 * slow * fast
    kept = slow + 1
    padded = -(-kept // 8) * 8
    k1 = np.arange(kept)
    n1 = np.arange(slow)
    n2 = np.arange(fast)
    angle1 = 2.0 * np.pi * (np.outer(k1, n1) % (2 * slow)) / (2 * slow)
    first = np.zeros((2 * padded, slow))
    first[:kept] = np.cos(angle1)
    first[padded : padded + kept] = -np.sin(angle1)
    angle2 = 2.0 * np.pi * (np.outer(k1, n2) % length) / length
    twiddle = np.zeros((2, padded, fast))
    twiddle[0, :kept] = np.cos(angle2)
    twiddle[1, :kept] = -np.sin(angle2)
    angle3 = 2.0 * np.pi * (np.outer(n2, n2) % fast) / fast
    cosine, sine = np.cos(angle3), np.sin(angle3)
    ahead = np.block([[cosine, -sine], [sine, cosine]])
    back = np.block([[cosine, sine], [-sine, cosine]])
    weight = np.where((k1 == 0) | (k1 == slow), 1.0, 2.0)[:, None] * (factor / length)
    last = np.zeros((slow, 2 * padded))
    last[:, :kept] = (weight * np.cos(angle1)).T
    last[:, padded : padded + kept] = (-weight * np.sin(angle1)).T
    return padded, first, twiddle, ahead, back, last


def before_kernel(q_ref, k_ref, v_ref, g_ref, w_ref, sig_ref, tap_ref):
    seq_parts, _, pieces, group, fast = sig_ref.shape
    for u in range(pieces):
        rows = pl.ds(u * fast, fast)
        mixed_in = k_ref[rows, :].astype(F32) * v_ref[rows, :].astype(F32)
        gate_grad = g_ref[rows, :].astype(F32) * q_ref[rows, :].astype(F32)
        for slot, part in enumerate((mixed_in, gate_grad)):
            turned = part.T
            for t in range(seq_parts):
                sig_ref[t, slot, u] = turned[t * group : (t + 1) * group].astype(BF16)
    width = seq_parts * group
    for a in range(w_ref.shape[1] // width):
        turned = w_ref[:, a * width : (a + 1) * width].astype(F32).T
        for t in range(seq_parts):
            tap_ref[a * seq_parts + t] = turned[t * group : (t + 1) * group].astype(BF16)


def exchange_kernel(
    n_chan, n_seq, to_taps, sig_ref, tap_ref, out_sig, out_tap, own_sem, s_send, s_recv, t_send, t_recv
):
    a, s = lax.axis_index("chan"), lax.axis_index("seq")
    n_all = n_chan * n_seq
    me = a * n_seq + s

    def place(index):
        return index // n_seq, index % n_seq

    def signal_id(index):
        return index

    def block_id(index):
        chan, seq = place(index)
        return seq * n_chan + chan

    source_slot, landing_slot = (signal_id, block_id) if to_taps else (block_id, signal_id)

    barrier = pltpu.get_barrier_semaphore()

    def greet(d, carry):
        pl.semaphore_signal(
            barrier, inc=1, device_id=place(lax.rem(me + d, n_all)), device_id_type=MESH
        )
        return carry

    lax.fori_loop(1, n_all, greet, 0)
    own_sig = pltpu.make_async_copy(sig_ref.at[s], out_sig.at[s], own_sem.at[0])
    own_tap = pltpu.make_async_copy(
        tap_ref.at[source_slot(me)], out_tap.at[landing_slot(me)], own_sem.at[1]
    )
    own_sig.start()
    own_tap.start()
    pl.semaphore_wait(barrier, n_all - 1)

    def sig_copy(d, landing):
        there = lax.rem(s + d, n_seq)
        return pltpu.make_async_remote_copy(
            src_ref=sig_ref.at[there],
            dst_ref=out_sig.at[landing],
            send_sem=s_send.at[d],
            recv_sem=s_recv.at[d],
            device_id=(a, there),
            device_id_type=MESH,
        )

    def tap_copy(d, landing):
        there = lax.rem(me + d, n_all)
        return pltpu.make_async_remote_copy(
            src_ref=tap_ref.at[source_slot(there)],
            dst_ref=out_tap.at[landing],
            send_sem=t_send.at[d],
            recv_sem=t_recv.at[d],
            device_id=place(there),
            device_id_type=MESH,
        )

    def start_sig(d, carry):
        sig_copy(d, s).start()
        return carry

    def start_tap(d, carry):
        tap_copy(d, landing_slot(me)).start()
        return carry

    lax.fori_loop(1, n_seq, start_sig, 0)
    lax.fori_loop(1, n_all, start_tap, 0)

    def wait_sig(d, carry):
        sig_copy(d, lax.rem(s + n_seq - d, n_seq)).wait()
        return carry

    def wait_tap(d, carry):
        tap_copy(d, landing_slot(lax.rem(me + n_all - d, n_all))).wait()
        return carry

    own_sig.wait()
    own_tap.wait()
    lax.fori_loop(1, n_seq, wait_sig, 0)
    lax.fori_loop(1, n_all, wait_tap, 0)


def exchange(n_chan, n_seq, to_taps, sig, taps):
    n_all = n_chan * n_seq
    return pl.pallas_call(
        functools.partial(exchange_kernel, n_chan, n_seq, to_taps),
        out_shape=[
            jax.ShapeDtypeStruct(sig.shape, sig.dtype),
            jax.ShapeDtypeStruct(taps.shape, taps.dtype),
        ],
        in_specs=whole_vmem(2),
        out_specs=whole_vmem(2),
        scratch_shapes=[
            pltpu.SemaphoreType.DMA((2,)),
            pltpu.SemaphoreType.DMA((n_seq,)),
            pltpu.SemaphoreType.DMA((n_seq,)),
            pltpu.SemaphoreType.DMA((n_all,)),
            pltpu.SemaphoreType.DMA((n_all,)),
        ],
        compiler_params=pltpu.CompilerParams(
            collective_id=0 if to_taps else 1, has_side_effects=True
        ),
        name="spread" if to_taps else "collect",
    )(sig, taps)


def conv_kernel(
    padded, sig_ref, tap_ref, first_h, first_l, twid_ref, ahead_h, ahead_l, back_h, back_l, last_h, last_l,
    out_sig, out_tap, lines, turned, spec,
):
    seq_parts, _, pieces, group, fast = sig_ref.shape
    slow = seq_parts * pieces
    for s in range(seq_parts):
        for u in range(pieces):
            row = s * pieces + u
            at = pl.ds(row * group, group)
            lines[0, at, :] = sig_ref[s, 0, u].astype(F32)
            lines[1, at, :] = sig_ref[s, 1, u].astype(F32)
            lines[2, at, :] = tap_ref[row].astype(F32)
    cosine, sine = twid_ref[0], twid_ref[1]
    for slot in range(3):
        for c in range(group):
            column = lines[slot, pl.ds(c, slow, stride=group), :].astype(BF16)
            got = dot(first_h[...], column) + dot(first_l[...], column)
            real, imag = got[:padded], got[padded:]
            at = pl.ds(c * padded, padded)
            turned[slot, at, :fast] = real * cosine - imag * sine
            turned[slot, at, fast:] = real * sine + imag * cosine

    def through(x, high, low):
        x_high, x_low = split_value(x)
        return dot(x_high, high[...]) + dot(x_low, high[...]) + dot(x_high, low[...])

    for c in range(group):
        at = pl.ds(c * padded, padded)
        lists = []
        for slot in range(3):
            line = through(turned[slot, at, :], ahead_h, ahead_l)
            lists.append((line[:, :fast], line[:, fast:]))
        (xr, xi), (gr, gi), (fr, fi) = lists
        spec[0, at, :fast] = fr * xr - fi * xi
        spec[0, at, fast:] = fr * xi + fi * xr
        spec[1, at, :fast] = fr * gr + fi * gi
        spec[1, at, fast:] = fr * gi - fi * gr
        spec[2, at, :fast] = xr * gr + xi * gi
        spec[2, at, fast:] = xr * gi - xi * gr
    for c in range(group):
        at = pl.ds(c * padded, padded)
        for slot in range(3):
            line = through(spec[slot, at, :], back_h, back_l)
            real, imag = line[:, :fast], line[:, fast:]
            both = jnp.concatenate(
                [real * cosine + imag * sine, imag * cosine - real * sine], axis=0
            )
            both_h, both_l = split_value(both)
            lines[slot, pl.ds(c, slow, stride=group), :] = (
                dot(last_h[...], both_h) + dot(last_h[...], both_l) + dot(last_l[...], both_h)
            )
    for s in range(seq_parts):
        for u in range(pieces):
            row = s * pieces + u
            at = pl.ds(row * group, group)
            out_sig[s, 0, u] = lines[0, at, :].astype(BF16)
            out_sig[s, 1, u] = lines[1, at, :].astype(BF16)
            out_tap[row] = lines[2, at, :].astype(BF16)


def after_kernel(
    q_ref, k_ref, v_ref, g_ref, gain_ref, sig_ref, tap_ref, m_ref, qg_ref, kg_ref, vg_ref, fg_ref, hold
):
    seq_parts, _, pieces, group, fast = sig_ref.shape
    width = seq_parts * group
    gain = gain_ref[...]

    def columns(pick):
        for t in range(seq_parts):
            hold[pl.ds(t * group, group), :] = pick(t).astype(F32)
        return hold[...].T

    for u in range(pieces):
        rows = pl.ds(u * fast, fast)
        query, key = q_ref[rows, :].astype(F32), k_ref[rows, :].astype(F32)
        value, grad = v_ref[rows, :].astype(F32), g_ref[rows, :].astype(F32)
        state = columns(lambda t: sig_ref[t, 0, u]) + gain * (key * value)
        m_ref[rows, :] = (query * state).astype(BF16)
        qg_ref[rows, :] = (grad * state).astype(BF16)
        back = columns(lambda t: sig_ref[t, 1, u]) + gain * (grad * query)
        kg_ref[rows, :] = (back * value).astype(BF16)
        vg_ref[rows, :] = (back * key).astype(BF16)
    for a in range(tap_ref.shape[0] // seq_parts):
        fg_ref[:, a * width : (a + 1) * width] = columns(lambda t: tap_ref[a * seq_parts + t])


def body(n_chan, n_seq, query, key, value, filter_weights, skip_gain, cotangent):
    rows, width = query.shape
    tap_rows, _, all_width = filter_weights.shape
    fast, group, pieces, n_all = tap_rows, width // n_seq, n_chan, n_chan * n_seq
    slow = rows * n_seq // fast
    padded, first, twiddle, ahead, back, last = tables(slow, fast, 1.0 / math.sqrt(rows * n_seq))
    weights = filter_weights.reshape(tap_rows, all_width)
    sig_shape = jax.ShapeDtypeStruct((n_seq, 2, pieces, group, fast), BF16)
    tap_shape = jax.ShapeDtypeStruct((n_all, group, fast), BF16)
    limit = pltpu.CompilerParams(vmem_limit_bytes=60 * 1024 * 1024)
    sig, taps = pl.pallas_call(
        before_kernel,
        out_shape=[sig_shape, tap_shape],
        in_specs=whole_vmem(5),
        out_specs=whole_vmem(2),
        compiler_params=limit,
        name="before",
    )(query, key, value, cotangent, weights)
    sig, taps = exchange(n_chan, n_seq, True, sig, taps)
    consts = [*split_table(first), jnp.asarray(twiddle, F32)]
    for table in (ahead, back, last):
        consts += split_table(table)
    sig, taps = pl.pallas_call(
        functools.partial(conv_kernel, padded),
        out_shape=[sig_shape, tap_shape],
        in_specs=whole_vmem(2 + len(consts)),
        out_specs=whole_vmem(2),
        scratch_shapes=[
            pltpu.VMEM((3, slow * group, fast), F32),
            pltpu.VMEM((3, group * padded, 2 * fast), F32),
            pltpu.VMEM((3, group * padded, 2 * fast), F32),
        ],
        compiler_params=limit,
        name="conv",
    )(sig, taps, *consts)
    sig, taps = exchange(n_chan, n_seq, False, sig, taps)
    flat = jax.ShapeDtypeStruct((rows, width), BF16)
    outs = pl.pallas_call(
        after_kernel,
        out_shape=[flat, flat, flat, flat, jax.ShapeDtypeStruct((tap_rows, all_width), F32)],
        in_specs=whole_vmem(7),
        out_specs=whole_vmem(5),
        scratch_shapes=[pltpu.VMEM((width, fast), F32)],
        compiler_params=limit,
        name="after",
    )(query, key, value, cotangent, skip_gain.reshape(1, width), sig, taps)
    return (*outs[:4], outs[4].reshape(tap_rows, 1, all_width))


def solution(mesh):
    n_chan, n_seq = mesh.shape["chan"], mesh.shape["seq"]
    block = P("seq", "chan")
    taps = P("chan", "seq", None)
    return jax.shard_map(
        functools.partial(body, n_chan, n_seq),
        mesh=mesh,
        in_specs=(block, block, block, taps, P("chan"), block),
        out_specs=(block, block, block, block, taps),
        check_vma=False,
    )
```

profile of v0, /device:TPU:0, one launch (start us, length us, event | category | flops | bytes accessed | tf_op | source)
XLA Modules:
  0.0 61.3 jit_solution(13327212065037068617)
XLA Ops:
  0.6 2.1 %before.1 = (bf16[8,2,4,16,128]{4,3,2,1,0:T(8,128)(2,1)}, bf16[32,16,128]{2,1,0:T(8,128)(2,1)}) custom-call(bf16[512,128]{1,0:T(8,128)(2,1)} %q_ref.3, bf16[512,128]{1,0:T(8,128)(2,1)} %k_ref.3, bf16[512,128]{1,0:T(8,128)(2,1)} %v_ref.3, bf16[512,128]{1,0:T(8,128)(2,1)} %g_ref.3, bf16[128,512]{1,0:T(8,128)(2,1)} %bitcast.4), custom_call_target="tpu_custom_call" | custom-call | tf_op jit(solution)/shard_map/before/pallas_call | solution.py:283
  2.7 19.4 %spread.1 = (bf16[8,2,4,16,128]{4,3,2,1,0:T(8,128)(2,1)}, bf16[32,16,128]{2,1,0:T(8,128)(2,1)}) custom-call(bf16[8,2,4,16,128]{4,3,2,1,0:T(8,128)(2,1)} %get-tuple-element.18.sig_ref, bf16[32,16,128]{2,1,0:T(8,128)(2,1)} %get-tuple-element.19.tap_ref), custom_call_target="tpu_custom_call" | custom-call | tf_op jit(solution)/shard_map/spread/pallas_call | solution.py:164
  22.1 18.5 %conv.1 = (bf16[8,2,4,16,128]{4,3,2,1,0:T(8,128)(2,1)}, bf16[32,16,128]{2,1,0:T(8,128)(2,1)}) custom-call(bf16[8,2,4,16,128]{4,3,2,1,0:T(8,128)(2,1)} %get-tuple-element.20.sig_ref, bf16[32,16,128]{2,1,0:T(8,128)(2,1)} %get-tuple-element.21.tap_ref, bf16[80,32]{1,0:T(8,128)(2,1)} %constant.16.first_h, bf16[80,32]{1,0:T(8,128)(2,1)} %constant.19.first_l, ...), custom_call_target="tpu_custom_call" | custom-call | tf_op jit(solution)/shard_map/conv/pallas_call | solution.py:295
  40.6 16.5 %collect.1 = (bf16[8,2,4,16,128]{4,3,2,1,0:T(8,128)(2,1)}, bf16[32,16,128]{2,1,0:T(8,128)(2,1)}) custom-call(bf16[8,2,4,16,128]{4,3,2,1,0:T(8,128)(2,1)} %get-tuple-element.22.sig_ref, bf16[32,16,128]{2,1,0:T(8,128)(2,1)} %get-tuple-element.23.tap_ref), custom_call_target="tpu_custom_call" | custom-call | tf_op jit(solution)/shard_map/collect/pallas_call | solution.py:164
  57.1 2.3 %after.1 = (bf16[512,128]{1,0:T(8,128)(2,1)}, bf16[512,128]{1,0:T(8,128)(2,1)}, bf16[512,128]{1,0:T(8,128)(2,1)}, bf16[512,128]{1,0:T(8,128)(2,1)}, f32[128,512]{1,0:T(8,128)}) custom-call(bf16[512,128]{1,0:T(8,128)(2,1)} %q_ref.3, bf16[512,128]{1,0:T(8,128)(2,1)} %k_ref.3, bf16[512,128]{1,0:T(8,128)(2,1)} %v_ref.3, bf16[512,128]{1,0:T(8,128)(2,1)} %g_ref.3, ...), custom_call_target="tpu_custom_call" | custom-call | tf_op jit(solution)/shard_map/after/pallas_call | solution.py:310
  59.4 1.9 %copy.20 = f32[128,1,512]{2,1,0:T(1,128)} copy(f32[128,1,512]{2,0,1:T(8,128)} %bitcast.3) | data formatting | bytes 524288
where the time goes:
time: 61.6 us; the launch traced here: 61.3 us
  Pallas kernels  58.8 us (95%)
  local copies, waits for them, and re-layouts  1.92 us (3%)
  between operations  0.65 us (1%)
    pallas_call x2, Pallas kernels, exchange(): pl.pallas_call(functools.partial(exchange_kernel, n_chan, n_seq, to_taps)...  35.9 us
    pallas_call x1, Pallas kernels, body(): pl.pallas_call(functools.partial(conv_kernel, padded), out_shape=[sig_sha...  18.5 us
    pallas_call x1, Pallas kernels, body(): pl.pallas_call(after_kernel, out_shape=[flat, flat, flat, flat, jax.Shape...  2.29 us
    pallas_call x1, Pallas kernels, body(): pl.pallas_call(before_kernel, out_shape=[sig_shape, tap_shape], in_specs=...  2.05 us
    unnamed x1, local copies, waits for them, and re-layouts  1.92 us

commit v1 on v0

v1 whole, which is shorter than its diff:
```python
import functools
import math

import jax
import jax.numpy as jnp
import numpy as np
from jax import lax
from jax.experimental import pallas as pl
from jax.experimental.pallas import tpu as pltpu
from jax.sharding import PartitionSpec as P

MESH = pl.DeviceIdType.MESH
F32 = jnp.float32
BF16 = jnp.bfloat16


def whole_vmem(count):
    return [pl.BlockSpec(memory_space=pltpu.VMEM)] * count


def split_table(table):
    high = jnp.asarray(table, F32).astype(BF16)
    low = (jnp.asarray(table, F32) - high.astype(F32)).astype(BF16)
    return high, low


def dot(a, b):
    return jnp.dot(a, b, preferred_element_type=F32)


def tables(slow, fast, factor):
    length = 2 * slow * fast
    kept = slow + 1
    padded = -(-kept // 8) * 8
    k1 = np.arange(kept)
    n1 = np.arange(slow)
    n2 = np.arange(fast)
    angle1 = 2.0 * np.pi * (np.outer(k1, n1) % (2 * slow)) / (2 * slow)
    first = np.zeros((2 * padded, slow))
    first[:kept] = np.cos(angle1)
    first[padded : padded + kept] = -np.sin(angle1)
    angle2 = 2.0 * np.pi * (np.outer(k1, n2) % length) / length
    twiddle = np.zeros((2, padded, fast))
    twiddle[0, :kept] = np.cos(angle2)
    twiddle[1, :kept] = -np.sin(angle2)
    angle3 = 2.0 * np.pi * (np.outer(n2, n2) % fast) / fast
    cosine, sine = np.cos(angle3), np.sin(angle3)
    ahead = np.block([[cosine, -sine], [sine, cosine]])
    back = np.block([[cosine, sine], [-sine, cosine]])
    weight = np.where((k1 == 0) | (k1 == slow), 1.0, 2.0)[:, None] * (factor / length)
    last = np.zeros((slow, 2 * padded))
    last[:, :kept] = (weight * np.cos(angle1)).T
    last[:, padded : padded + kept] = (-weight * np.sin(angle1)).T
    return padded, first, twiddle, ahead, back, last


def core_kernel(
    n_chan, n_seq, padded,
    q_ref, k_ref, v_ref, g_ref, w_ref, first_ref, twid_ref, ahead_h, ahead_l, back_h, back_l, last_ref,
    out_sig, out_tap,
    send_sig, send_tap, in_sig, in_tap, res_sig, res_tap, lines, turned, spec,
    own_sem, s_send, s_recv, t_send, t_recv, rs_send, rs_recv, rt_send, rt_recv,
):
    chan, seq = lax.axis_index("chan"), lax.axis_index("seq")
    n_all = n_chan * n_seq
    me = chan * n_seq + seq
    _, chunks, _, pieces, part, fast = send_sig.shape
    group = chunks * part
    slow = n_seq * pieces
    width = n_seq * group

    def place(index):
        return index // n_seq, index % n_seq

    def block_of(index):
        at_chan, at_seq = place(index)
        return at_seq * n_chan + at_chan

    barrier = pltpu.get_barrier_semaphore()

    def greet(d, carry):
        pl.semaphore_signal(
            barrier, inc=1, device_id=place(lax.rem(me + d, n_all)), device_id_type=MESH
        )
        return carry

    lax.fori_loop(1, n_all, greet, 0)

    for u in range(pieces):
        rows = pl.ds(u * fast, fast)
        mixed_in = k_ref[rows, :].astype(F32) * v_ref[rows, :].astype(F32)
        gate_grad = g_ref[rows, :].astype(F32) * q_ref[rows, :].astype(F32)
        for slot, signal in enumerate((mixed_in, gate_grad)):
            flipped = signal.T
            for t in range(n_seq):
                for q in range(chunks):
                    low = t * group + q * part
                    send_sig[t, q, slot, u] = flipped[low : low + part].astype(BF16)
    for a in range(n_chan):
        flipped = w_ref[:, a * width : (a + 1) * width].astype(F32).T
        for t in range(n_seq):
            send_tap[a * n_seq + t] = flipped[t * group : (t + 1) * group].astype(BF16)

    def remote(source, target, send, recv, device):
        return pltpu.make_async_remote_copy(
            src_ref=source, dst_ref=target, send_sem=send, recv_sem=recv,
            device_id=device, device_id_type=MESH,
        )

    def sig_copy(q, d, landing, ahead):
        there = lax.rem(seq + d, n_seq)
        source, target = (send_sig, in_sig) if ahead else (res_sig, out_sig)
        send, recv = (s_send, s_recv) if ahead else (rs_send, rs_recv)
        return remote(
            source.at[there, q], target.at[landing, q], send.at[q, d], recv.at[q, d], (chan, there)
        )

    def tap_copy(d, landing):
        there = lax.rem(me + d, n_all)
        return remote(
            send_tap.at[there], in_tap.at[landing], t_send.at[d], t_recv.at[d], place(there)
        )

    def grad_copy(q, d, landing):
        there = lax.rem(me + d, n_all)
        return remote(
            res_tap.at[q, block_of(there)], out_tap.at[q, landing],
            rt_send.at[q, d], rt_recv.at[q, d], place(there),
        )

    def each(count, act):
        def step(d, carry):
            act(d)
            return carry

        lax.fori_loop(1, count, step, 0)

    def seq_from(d):
        return lax.rem(seq + n_seq - d, n_seq)

    def all_from(d):
        return lax.rem(me + n_all - d, n_all)

    own = [pltpu.make_async_copy(send_tap.at[me], in_tap.at[block_of(me)], own_sem.at[0])]
    for q in range(chunks):
        own.append(
            pltpu.make_async_copy(send_sig.at[seq, q], in_sig.at[seq, q], own_sem.at[1 + q])
        )

    pl.semaphore_wait(barrier, n_all - 1)
    each(n_seq, lambda d: sig_copy(0, d, seq, True).start())
    each(n_all, lambda d: tap_copy(d, block_of(me)).start())
    for q in range(1, chunks):
        each(n_seq, lambda d: sig_copy(q, d, seq, True).start())
    for copy in own:
        copy.start()

    cosine, sine = twid_ref[0], twid_ref[1]
    joint = fast % 128 == 0 and part % 2 == 0
    batch = 2 if joint else 1

    def times(table, columns):
        if not joint:
            return [dot(table, column) for column in columns]
        wide = dot(table, jnp.concatenate(columns, axis=1))
        return [wide[:, i * fast : (i + 1) * fast] for i in range(len(columns))]

    def through(x, high, low):
        short = x.astype(BF16)
        return dot(short, high[...]) + dot(short, low[...])

    def transform(q):
        for s in range(n_seq):
            for u in range(pieces):
                row = s * pieces + u
                at = pl.ds(row * part, part)
                lines[0, at, :] = in_sig[s, q, 0, u].astype(F32)
                lines[1, at, :] = in_sig[s, q, 1, u].astype(F32)
                lines[2, at, :] = in_tap[row, q * part : (q + 1) * part].astype(F32)
        for base in range(0, part, batch):
            picks = [(slot, c) for c in range(base, base + batch) for slot in range(3)]
            columns = []
            for slot, c in picks:
                column = lines[slot, pl.ds(c, slow, stride=part), :].astype(BF16)
                columns.append(jnp.concatenate([column, column], axis=0))
            for (slot, c), got in zip(picks, times(first_ref[...], columns)):
                real, imag = got[:padded], got[padded:]
                at = pl.ds(c * padded, padded)
                turned[slot, at, :fast] = real * cosine - imag * sine
                turned[slot, at, fast:] = real * sine + imag * cosine
        for slot in range(3):
            turned[slot] = through(turned[slot], ahead_h, ahead_l)
        for c in range(part):
            at = pl.ds(c * padded, padded)
            xr, xi = turned[0, at, :fast], turned[0, at, fast:]
            gr, gi = turned[1, at, :fast], turned[1, at, fast:]
            fr, fi = turned[2, at, :fast], turned[2, at, fast:]
            spec[0, at, :fast] = fr * xr - fi * xi
            spec[0, at, fast:] = fr * xi + fi * xr
            spec[1, at, :fast] = fr * gr + fi * gi
            spec[1, at, fast:] = fr * gi - fi * gr
            spec[2, at, :fast] = xr * gr + xi * gi
            spec[2, at, fast:] = xr * gi - xi * gr
        for slot in range(3):
            spec[slot] = through(spec[slot], back_h, back_l)
        for base in range(0, part, batch):
            picks = [(slot, c) for c in range(base, base + batch) for slot in range(3)]
            columns = []
            for slot, c in picks:
                at = pl.ds(c * padded, padded)
                real, imag = spec[slot, at, :fast], spec[slot, at, fast:]
                real, imag = real * cosine + imag * sine, imag * cosine - real * sine
                both = jnp.concatenate([real, imag], axis=0).astype(BF16)
                columns.append(jnp.concatenate([both, both], axis=0))
            for (slot, c), got in zip(picks, times(last_ref[...], columns)):
                lines[slot, pl.ds(c, slow, stride=part), :] = got
        for s in range(n_seq):
            for u in range(pieces):
                row = s * pieces + u
                at = pl.ds(row * part, part)
                res_sig[s, q, 0, u] = lines[0, at, :].astype(BF16)
                res_sig[s, q, 1, u] = lines[1, at, :].astype(BF16)
                res_tap[q, row] = lines[2, at, :].astype(BF16)

    own[0].wait()
    for q in range(chunks):
        own[1 + q].wait()
        each(n_seq, lambda d: sig_copy(q, d, seq_from(d), True).wait())
        if q == 0:
            each(n_all, lambda d: tap_copy(d, block_of(all_from(d))).wait())
        transform(q)
        each(n_seq, lambda d: sig_copy(q, d, seq, False).start())
        each(n_all, lambda d: grad_copy(q, d, me).start())
        for copy in (
            pltpu.make_async_copy(res_sig.at[seq, q], out_sig.at[seq, q], own_sem.at[1 + chunks + q]),
            pltpu.make_async_copy(
                res_tap.at[q, block_of(me)], out_tap.at[q, me], own_sem.at[1 + 2 * chunks + q]
            ),
        ):
            copy.start()
            own.append(copy)
    for copy in own[1 + chunks :]:
        copy.wait()
    for q in range(chunks):
        each(n_seq, lambda d: sig_copy(q, d, seq_from(d), False).wait())
        each(n_all, lambda d: grad_copy(q, d, all_from(d)).wait())


def after_kernel(
    q_ref, k_ref, v_ref, g_ref, gain_ref, sig_ref, tap_ref, m_ref, qg_ref, kg_ref, vg_ref, fg_ref, hold
):
    seq_parts, chunks, _, pieces, part, fast = sig_ref.shape
    group = chunks * part
    gain = gain_ref[...]

    def columns(pick):
        for t in range(seq_parts):
            for q in range(chunks):
                hold[pl.ds(t * group + q * part, part), :] = pick(t, q).astype(F32)
        return hold[...].T

    for u in range(pieces):
        rows = pl.ds(u * fast, fast)
        query, key = q_ref[rows, :].astype(F32), k_ref[rows, :].astype(F32)
        value, grad = v_ref[rows, :].astype(F32), g_ref[rows, :].astype(F32)
        state = columns(lambda t, q: sig_ref[t, q, 0, u]) + gain * (key * value)
        m_ref[rows, :] = (query * state).astype(BF16)
        qg_ref[rows, :] = (grad * state).astype(BF16)
        back = columns(lambda t, q: sig_ref[t, q, 1, u]) + gain * (grad * query)
        kg_ref[rows, :] = (back * value).astype(BF16)
        vg_ref[rows, :] = (back * key).astype(BF16)
    for a in range(pieces):
        got = columns(lambda t, q: tap_ref[q, a * seq_parts + t])
        fg_ref[pl.ds(a, fast, stride=pieces), :] = got


def body(n_chan, n_seq, query, key, value, filter_weights, skip_gain, cotangent):
    rows, width = query.shape
    tap_rows, _, all_width = filter_weights.shape
    fast, group, pieces, n_all = tap_rows, width // n_seq, n_chan, n_chan * n_seq
    slow = rows * n_seq // fast
    chunks = 2 if group % 16 == 0 else 1
    part = group // chunks
    padded, first, twiddle, ahead, back, last = tables(slow, fast, 1.0 / math.sqrt(rows * n_seq))
    weights = filter_weights.reshape(tap_rows, all_width)
    consts = [
        jnp.concatenate(split_table(first), axis=1),
        jnp.asarray(twiddle, F32),
        *split_table(ahead),
        *split_table(back),
        jnp.concatenate(split_table(last), axis=1),
    ]
    sig_dims = (n_seq, chunks, 2, pieces, part, fast)
    grad_dims = (chunks, n_all, part, fast)
    tap_dims = (n_all, group, fast)
    dma = pltpu.SemaphoreType.DMA
    sig, taps = pl.pallas_call(
        functools.partial(core_kernel, n_chan, n_seq, padded),
        out_shape=[jax.ShapeDtypeStruct(sig_dims, BF16), jax.ShapeDtypeStruct(grad_dims, BF16)],
        in_specs=whole_vmem(5 + len(consts)),
        out_specs=whole_vmem(2),
        scratch_shapes=[
            pltpu.VMEM(sig_dims, BF16),
            pltpu.VMEM(tap_dims, BF16),
            pltpu.VMEM(sig_dims, BF16),
            pltpu.VMEM(tap_dims, BF16),
            pltpu.VMEM(sig_dims, BF16),
            pltpu.VMEM(grad_dims, BF16),
            pltpu.VMEM((3, slow * part, fast), F32),
            pltpu.VMEM((3, part * padded, 2 * fast), F32),
            pltpu.VMEM((3, part * padded, 2 * fast), F32),
            dma((1 + 3 * chunks,)),
            dma((chunks, n_seq)),
            dma((chunks, n_seq)),
            dma((n_all,)),
            dma((n_all,)),
            dma((chunks, n_seq)),
            dma((chunks, n_seq)),
            dma((chunks, n_all)),
            dma((chunks, n_all)),
        ],
        compiler_params=pltpu.CompilerParams(
            collective_id=0, has_side_effects=True, vmem_limit_bytes=60 * 1024 * 1024
        ),
        name="core",
    )(query, key, value, cotangent, weights, *consts)
    flat = jax.ShapeDtypeStruct((rows, width), BF16)
    outs = pl.pallas_call(
        after_kernel,
        out_shape=[flat, flat, flat, flat, jax.ShapeDtypeStruct((tap_rows * n_chan, width), F32)],
        in_specs=whole_vmem(7),
        out_specs=whole_vmem(5),
        scratch_shapes=[pltpu.VMEM((width, fast), F32)],
        compiler_params=pltpu.CompilerParams(vmem_limit_bytes=60 * 1024 * 1024),
        name="after",
    )(query, key, value, cotangent, skip_gain.reshape(1, width), sig, taps)
    return (*outs[:4], outs[4].reshape(tap_rows, 1, all_width))


def solution(mesh):
    n_chan, n_seq = mesh.shape["chan"], mesh.shape["seq"]
    block = P("seq", "chan")
    taps = P("chan", "seq", None)
    return jax.shard_map(
        functools.partial(body, n_chan, n_seq),
        mesh=mesh,
        in_specs=(block, block, block, taps, P("chan"), block),
        out_specs=(block, block, block, block, taps),
        check_vma=False,
    )
```

time: 61.6 us -> 36.6 us (0.59)
  Pallas kernels: 58.8 us -> 35.8 us
  local copies, waits for them, and re-layouts: 1.92 us -> 0 us
    pallas_call x4 -> x1, Pallas kernels: 56.5 us -> 33.5 us  [body(): pl.pallas_call(functools.partial(core_kernel, n_chan, n_seq, padded), out...]
    unnamed x1 -> x0, local copies, waits for them, and re-layouts: 1.92 us -> none
where the time goes in v1:
time: 36.6 us; the launch traced here: 36.4 us
  Pallas kernels  35.8 us (98%)
  between operations  0.64 us (2%)
    pallas_call x1, Pallas kernels, body(): pl.pallas_call(functools.partial(core_kernel, n_chan, n_seq, padded), out...  33.5 us
    pallas_call x1, Pallas kernels, body(): pl.pallas_call(after_kernel, out_shape=[flat, flat, flat, flat, jax.Shape...  2.3 us

profile of v1, /device:TPU:0, one launch (start us, length us, event | category | flops | bytes accessed | tf_op | source)
XLA Modules:
  0.0 36.4 jit_solution(4119899742811471400)
XLA Ops:
  0.6 33.5 %core.1 = (bf16[8,2,2,4,8,128]{5,4,3,2,1,0:T(8,128)(2,1)}, bf16[2,32,8,128]{3,2,1,0:T(8,128)(2,1)}) custom-call(bf16[512,128]{1,0:T(8,128)(2,1)} %q_ref.3, bf16[512,128]{1,0:T(8,128)(2,1)} %k_ref.3, bf16[512,128]{1,0:T(8,128)(2,1)} %v_ref.3, bf16[512,128]{1,0:T(8,128)(2,1)} %g_ref.3, bf16[128,512]{1,0:T(8,128)(2,1)} %bitcast.3, ...), custom_call_target="tpu_custom_call" | custom-call | tf_op jit(solution)/shard_map/core/pallas_call | solution.py:297
  34.1 2.3 %after.1 = (bf16[512,128]{1,0:T(8,128)(2,1)}, bf16[512,128]{1,0:T(8,128)(2,1)}, bf16[512,128]{1,0:T(8,128)(2,1)}, bf16[512,128]{1,0:T(8,128)(2,1)}, f32[512,128]{1,0:T(8,128)}) custom-call(bf16[512,128]{1,0:T(8,128)(2,1)} %q_ref.3, bf16[512,128]{1,0:T(8,128)(2,1)} %k_ref.3, bf16[512,128]{1,0:T(8,128)(2,1)} %v_ref.3, bf16[512,128]{1,0:T(8,128)(2,1)} %g_ref.3, ...), custom_call_target="tpu_custom_call" | custom-call | tf_op jit(solution)/shard_map/after/pallas_call | solution.py:328

commit v2 on v1

--- a/solution.py
+++ b/solution.py
@@ -296,7 +296,7 @@
     dma = pltpu.SemaphoreType.DMA
     sig, taps = pl.pallas_call(
         functools.partial(core_kernel, n_chan, n_seq, padded),
-        out_shape=[jax.ShapeDtypeStruct(sig_dims, BF16), jax.ShapeDtypeStruct(grad_dims, BF16)],
+        out_shape=[pltpu.VMEM(sig_dims, BF16), pltpu.VMEM(grad_dims, BF16)],
         in_specs=whole_vmem(5 + len(consts)),
         out_specs=whole_vmem(2),
         scratch_shapes=[
@@ -331,7 +331,7 @@
         in_specs=whole_vmem(7),
         out_specs=whole_vmem(5),
         scratch_shapes=[pltpu.VMEM((width, fast), F32)],
-        compiler_params=pltpu.CompilerParams(vmem_limit_bytes=60 * 1024 * 1024),
+        compiler_params=pltpu.CompilerParams(vmem_limit_bytes=24 * 1024 * 1024),
         name="after",
     )(query, key, value, cotangent, skip_gain.reshape(1, width), sig, taps)
     return (*outs[:4], outs[4].reshape(tap_rows, 1, all_width))

time: 36.6 us -> 35.4 us (0.967)
  Pallas kernels: 35.8 us -> 33.9 us
  local copies, waits for them, and re-layouts: 0 us -> 0.63 us
    pallas_call x1, Pallas kernels: 2.3 us -> 1.08 us  [body(): pl.pallas_call(after_kernel, out_shape=[flat, flat, flat, flat, jax.Shape...]
    pallas_call x1, Pallas kernels: 33.5 us -> 32.8 us  [body(): pl.pallas_call(functools.partial(core_kernel, n_chan, n_seq, padded), out...]
    unnamed x0 -> x10, local copies, waits for them, and re-layouts: none -> 0.63 us
where the time goes in v2:
time: 35.4 us; the launch traced here: 35.2 us
  Pallas kernels  33.9 us (96%)
  between operations  0.71 us (2%)
  local copies, waits for them, and re-layouts  0.63 us (2%)
    pallas_call x1, Pallas kernels, body(): pl.pallas_call(functools.partial(core_kernel, n_chan, n_seq, padded), out...  32.8 us
    pallas_call x1, Pallas kernels, body(): pl.pallas_call(after_kernel, out_shape=[flat, flat, flat, flat, jax.Shape...  1.08 us

profile of v2, /device:TPU:0, one launch (start us, length us, event | category | flops | bytes accessed | tf_op | source)
XLA Modules:
  0.0 35.2 jit_solution(8295507744127420764)
XLA Ops:
  0.6 0.0 copy-start
  0.6 0.0 copy-start.1
  0.7 0.0 copy-start.2
  0.7 0.0 copy-start.3
  0.7 32.8 %core.1 = (bf16[8,2,2,4,8,128]{5,4,3,2,1,0:T(8,128)(2,1)S(1)}, bf16[2,32,8,128]{3,2,1,0:T(8,128)(2,1)S(1)}) custom-call(bf16[512,128]{1,0:T(8,128)(2,1)} %q_ref.3, bf16[512,128]{1,0:T(8,128)(2,1)} %k_ref.3, bf16[512,128]{1,0:T(8,128)(2,1)} %v_ref.3, bf16[512,128]{1,0:T(8,128)(2,1)} %g_ref.3, bf16[128,512]{1,0:T(8,128)(2,1)} %bitcast.4, ...), custom_call_target="tpu_custom_call" | custom-call | tf_op jit(solution)/shard_map/core/pallas_call | solution.py:297
  33.5 0.0 copy-start.4
  33.5 0.0 copy-done
  33.5 0.0 copy-done.1
  33.5 0.0 copy-done.2
  33.5 0.0 copy-done.3
  33.5 0.6 %copy-done.4 = f32[128]{0:T(128)S(1)} copy-done((f32[128]{0:T(128)S(1)}, f32[128]{0:T(128)}, u32[]{:S(2)}) %copy-start.4) | copy-done | bytes 536
  34.1 1.1 %after.1 = (bf16[512,128]{1,0:T(8,128)(2,1)}, bf16[512,128]{1,0:T(8,128)(2,1)}, bf16[512,128]{1,0:T(8,128)(2,1)}, bf16[512,128]{1,0:T(8,128)(2,1)}, f32[512,128]{1,0:T(8,128)}) custom-call(bf16[512,128]{1,0:T(8,128)(2,1)S(1)} %copy-done, bf16[512,128]{1,0:T(8,128)(2,1)S(1)} %copy-done.1, bf16[512,128]{1,0:T(8,128)(2,1)S(1)} %copy-done.2, ...), custom_call_target="tpu_custom_call" | custom-call | tf_op jit(solution)/shard_map/after/pallas_call | solution.py:328
Async XLA Ops:
  0.6 32.9 %copy-start = (bf16[512,128]{1,0:T(8,128)(2,1)S(1)}, bf16[512,128]{1,0:T(8,128)(2,1)}, u32[]{:S(2)}) copy-start(bf16[512,128]{1,0:T(8,128)(2,1)} %q_ref.3) | copy-start | bytes 393220
  0.6 32.9 %copy-start.1 = (bf16[512,128]{1,0:T(8,128)(2,1)S(1)}, bf16[512,128]{1,0:T(8,128)(2,1)}, u32[]{:S(2)}) copy-start(bf16[512,128]{1,0:T(8,128)(2,1)} %k_ref.3) | copy-start | bytes 393220
  0.7 32.9 %copy-start.2 = (bf16[512,128]{1,0:T(8,128)(2,1)S(1)}, bf16[512,128]{1,0:T(8,128)(2,1)}, u32[]{:S(2)}) copy-start(bf16[512,128]{1,0:T(8,128)(2,1)} %v_ref.3) | copy-start | bytes 393220
  0.7 32.9 %copy-start.3 = (bf16[512,128]{1,0:T(8,128)(2,1)S(1)}, bf16[512,128]{1,0:T(8,128)(2,1)}, u32[]{:S(2)}) copy-start(bf16[512,128]{1,0:T(8,128)(2,1)} %g_ref.3) | copy-start | bytes 393220
  33.5 0.7 %copy-start.4 = (f32[128]{0:T(128)S(1)}, f32[128]{0:T(128)}, u32[]{:S(2)}) copy-start(f32[128]{0:T(128)} %param.19) | copy-start | bytes 1540
